TPU v7x, 32 devices: a whole 2x2x4 slice. The times are simulated.
32 devices in a mesh: groups: 2 (over y), lon: 4 (over z), lat: 2 (over x), dp: 2 (over core).
Axes of the slice: x: 2, y: 2, z: 4, core: 2. Of those that a mesh axis runs over, the one named last changes fastest.
Arguments:
- inputs: bfloat16 [4, 128, 1024, 128], P(('groups', 'dp'), 'lat', 'lon'), parts along dimension 0, may hold values from -6 to 6
- cotangent: bfloat16 [4, 128, 1024, 128], P(('groups', 'dp'), 'lat', 'lon'), parts along dimension 0, may hold values from -6 to 6
- kernel_dw: bfloat16 [7, 7, 128], replicated, may hold values from -0.875 to 0.875
- bias_dw: float32 [128], replicated, may hold values from -3 to 3
- gain: float32 [128], replicated, may hold values from 0.1 to 1.9
- shift_ln: float32 [128], replicated, may hold values from -2 to 2
- w_in: bfloat16 [128, 256], replicated, may hold values from -0.5 to 0.5
- b_in: float32 [256], replicated, may hold values from -2 to 2
- w_out: bfloat16 [256, 128], replicated, may hold values from -0.375 to 0.375
- ocean_mask: int32 [2, 16], P('lat', 'lon'), may hold values from 0 to 1, as said below
Outputs:
- grad_inputs: bfloat16 [4, 128, 1024, 128], P(('groups', 'dp'), 'lat', 'lon'), parts along dimension 0
- grad_w_in: float32 [256, 256], P(('groups', 'dp')), parts along dimension 0
- grad_w_out: float32 [512, 128], P(('groups', 'dp')), parts along dimension 0
- grad_kernel: float32 [14, 7, 128], P('groups'), parts along dimension 0
- grad_bias_dw: float32 [256], P('groups'), parts along dimension 0
- grad_gain: float32 [256], P('groups'), parts along dimension 0
- grad_shift: float32 [256], P('groups'), parts along dimension 0
- grad_b_in: float32 [512], P('groups'), parts along dimension 0
There are 2 independent parts, one for each index of `groups`. A program takes and returns all parts, laid end to end along the dimension named above; an argument that names none is the same for every part. Nothing has to cross between parts.
Inputs may be any that keep to these rules, and one draw needn't show every extreme that they name: `ocean_mask`: every block of the northernmost block row (index 1) is ocean, and each aligned run of 4 blocks of a block row holds at least one ocean block.
All inputs are finite; a program needn't handle non-finite values.
Results may differ from a plain program's by a relative error of at most 0.0056.
Values may be sent and summed in bfloat16 or wider, within the bound.
A program may use at most 128 MiB of HBM per device.

v0:
```python
import math
import jax
import jax.numpy as jnp
from jax import lax
from jax.sharding import PartitionSpec as P

KS = 7
EPS = 1e-06
GELU_K = 0.7978845608
GELU_C = 0.044715


def padded(block, sides, width, periodic):
    for axis, dim in sides:
        count = lax.axis_size(axis)
        forward = [(i, i + 1) for i in range(count - 1)]
        if periodic:
            forward.append((count - 1, 0))
        backward = [(target, source) for source, target in forward]
        low = lax.ppermute(
            lax.slice_in_dim(block, block.shape[dim] - width, None, axis=dim), axis, forward
        )
        high = lax.ppermute(lax.slice_in_dim(block, 0, width, axis=dim), axis, backward)
        block = jnp.concatenate([low, block, high], axis=dim)
    return block


def partner(block, axis, stride):
    count = lax.axis_size(axis)
    route = []
    for low in range(count):
        high = low | 1 << stride
        if high != low and high < count:
            route += [(low, high), (high, low)]
    return lax.ppermute(block, axis, route)


def extend(field):
    half = KS // 2
    rows = field.shape[1]
    framed = padded(field, (("lat", 1),), half, False)
    mirror = field[:, rows - half :]
    for bit in range(lax.axis_size("lon").bit_length() - 1):
        mirror = partner(mirror, "lon", bit)
    band = mirror[:, ::-1, ::-1, :]
    northern = lax.axis_index("lat") == lax.axis_size("lat") - 1
    upper = jnp.where(northern, band, framed[:, rows + half :])
    framed = jnp.concatenate([framed[:, : rows + half], upper], 1)
    return padded(framed, (("lon", 2),), half, True)


def conv_valid(extended, kernel):
    return lax.conv_general_dilated(
        extended,
        kernel[:, :, None, :],
        (1, 1),
        "VALID",
        dimension_numbers=("NHWC", "HWIO", "NHWC"),
        feature_group_count=extended.shape[3],
        preferred_element_type=jnp.float32,
    )


def kernel_grad(extended, delta):
    out = lax.conv_general_dilated(
        extended[None],
        delta[:, :, None, :],
        (1, 1),
        "VALID",
        dimension_numbers=("NHWC", "HWIO", "NHWC"),
        feature_group_count=extended.shape[2],
        preferred_element_type=jnp.float32,
    )
    return out[0]


def cell_grads(ycells, gcells, maskval, gain, shift_ln, w_in, b_in, w_out):
    center = ycells - jnp.mean(ycells, -1, keepdims=True)
    rstd = lax.rsqrt(jnp.mean(center * center, -1, keepdims=True) + EPS)
    nhat = center * rstd
    normed = (nhat * gain + shift_ln).astype(jnp.bfloat16)
    pre = jnp.dot(normed, w_in, preferred_element_type=jnp.float32) + b_in
    tangent = jnp.tanh(GELU_K * (pre + GELU_C * pre * pre * pre))
    act = (0.5 * pre * (1.0 + tangent)).astype(jnp.bfloat16)
    outgrad = (gcells.astype(jnp.float32) * maskval).astype(jnp.bfloat16)
    g_out = lax.dot_general(
        act, outgrad, (((0,), (0,)), ((), ())), preferred_element_type=jnp.float32
    )
    dact = lax.dot_general(
        outgrad, w_out, (((1,), (1,)), ((), ())), preferred_element_type=jnp.float32
    )
    slope = 0.5 * (1.0 + tangent) + 0.5 * pre * (1.0 - tangent * tangent) * GELU_K * (
        1.0 + 3.0 * GELU_C * pre * pre
    )
    dpre = dact * slope
    dpre_b = dpre.astype(jnp.bfloat16)
    g_in = lax.dot_general(
        normed, dpre_b, (((0,), (0,)), ((), ())), preferred_element_type=jnp.float32
    )
    g_bin = jnp.sum(dpre, 0)
    dnorm = lax.dot_general(
        dpre_b, w_in, (((1,), (1,)), ((), ())), preferred_element_type=jnp.float32
    )
    g_gain = jnp.sum(dnorm * nhat, 0)
    g_shift = jnp.sum(dnorm, 0)
    dscaled = dnorm * gain
    delta = rstd * (
        dscaled
        - jnp.mean(dscaled, -1, keepdims=True)
        - nhat * jnp.mean(dscaled * nhat, -1, keepdims=True)
    )
    return (delta.astype(jnp.bfloat16), (g_in, g_bin, g_out, g_gain, g_shift))


def local(inputs, cotangent, kernel_dw, bias_dw, gain, shift_ln, w_in, b_in, w_out, ocean_mask):
    batch, rows, cols, chans = inputs.shape
    hidden = w_in.shape[1]
    half = KS // 2
    per_tile = cols // rows
    extended = extend(inputs)
    field_y = conv_valid(extended, kernel_dw) + bias_dw

    def to_blocks(field):
        parts = field.reshape(batch, rows, per_tile, rows, chans).transpose(0, 2, 1, 3, 4)
        return parts.reshape(batch * per_tile, rows * rows, chans)

    masks = jnp.tile(ocean_mask.reshape(-1), batch).astype(jnp.float32)
    totals = (
        jnp.zeros((chans, hidden), jnp.float32),
        jnp.zeros((hidden,), jnp.float32),
        jnp.zeros((hidden, chans), jnp.float32),
        jnp.zeros((chans,), jnp.float32),
        jnp.zeros((chans,), jnp.float32),
    )

    def step(carry, items):
        ycells, gcells, maskval = items
        delta, grads = cell_grads(ycells, gcells, maskval, gain, shift_ln, w_in, b_in, w_out)
        return (tuple((c + g for c, g in zip(carry, grads))), delta)

    totals, deltas = lax.scan(step, totals, (to_blocks(field_y), to_blocks(cotangent), masks))
    delta = (
        deltas.reshape(batch, per_tile, rows, rows, chans)
        .transpose(0, 2, 1, 3, 4)
        .reshape(batch, rows, cols, chans)
    )
    g_kernel = jnp.zeros((KS, KS, chans), jnp.float32)
    g_kernel = g_kernel + kernel_grad(extended[0], delta[0])
    g_bias = jnp.sum(delta.astype(jnp.float32), (0, 1, 2))
    spread = extend(delta)
    northern = lax.axis_index("lat") == lax.axis_size("lat") - 1
    fold_rows = spread[:, rows + half :]
    direct_part = jnp.concatenate(
        [spread[:, : rows + half], jnp.where(northern, jnp.zeros_like(fold_rows), fold_rows)], 1
    )
    direct = conv_valid(direct_part, kernel_dw[::-1, ::-1])
    fold_part = jnp.concatenate(
        [
            jnp.zeros_like(spread[:, rows - half : rows + half]),
            jnp.where(northern, fold_rows, jnp.zeros_like(fold_rows)),
        ],
        1,
    )
    fold = conv_valid(fold_part, kernel_dw)
    total = cotangent.astype(jnp.float32) + direct
    total = total.at[:, rows - half :].add(fold)
    grad_inputs = total.astype(jnp.bfloat16)
    g_in, g_bin, g_out, g_gain, g_shift = totals
    cells_all = (
        lax.axis_size("dp") * batch * lax.axis_size("lat") * rows * lax.axis_size("lon") * cols
    )
    scale = 1.0 / math.sqrt(cells_all)
    in_share = chans // lax.axis_size("dp")
    out_share = hidden // lax.axis_size("dp")
    summed = lax.psum((g_in, g_out, g_kernel, g_bias, g_gain, g_shift, g_bin), ("lon", "lat", "dp"))
    s_in, s_out, s_kernel, s_bias, s_gain, s_shift, s_bin = summed
    position = lax.axis_index("dp")
    s_in = lax.dynamic_slice_in_dim(s_in, position * in_share, in_share, 0)
    s_out = lax.dynamic_slice_in_dim(s_out, position * out_share, out_share, 0)
    return (
        grad_inputs,
        s_in * scale,
        s_out * scale,
        s_kernel * scale,
        s_bias * scale,
        s_gain * scale,
        s_shift * scale,
        s_bin * scale,
    )


def solution(mesh):
    placed = (
        P(("groups", "dp"), "lat", "lon", None),
        P(("groups", "dp"), "lat", "lon", None),
        P(),
        P(),
        P(),
        P(),
        P(),
        P(),
        P(),
        P("lat", "lon"),
    )
    return jax.shard_map(
        local,
        mesh=mesh,
        in_specs=placed,
        out_specs=(
            P(("groups", "dp"), "lat", "lon", None),
            P(("groups", "dp"), None),
            P(("groups", "dp"), None),
            P("groups", None, None),
            P("groups"),
            P("groups"),
            P("groups"),
            P("groups"),
        ),
        check_vma=False,
    )
```

profile of v0, /device:TPU:0, one launch (start us, length us, event | category | flops | bytes accessed | tf_op | source)
XLA Modules:
  0.0 606.1 jit_solution(1043596594227008258)
XLA Ops:
  7.2 7.8 %copy.54 = bf16[1,64,256,128]{3,0,2,1:T(2,128)(2,1)S(1)} copy(bf16[1,64,256,128]{3,2,1,0:T(8,128)(2,1)} %param.14) | data formatting | bytes 8388608 | tf_op args[0]
  23.4 7.8 %collective-permute-done.1 = bf16[1,3,256,128]{3,0,2,1:T(2,128)(2,1)S(1)} collective-permute-done((bf16[1,3,256,128]{3,0,2,1:T(2,128)(2,1)S(1)}, bf16[1,3,256,128]{3,0,2,1:T(2,128)(2,1)S(1)}, u32[]{:S(2)}, u32[]{:S(2)}) %collective-permute-start.1) | collective-permute-done | bytes 196640 | tf_op jit(solution)/shard_map/ppermute | solution.py:35
  37.4 13.4 %collective-permute-done.2 = bf16[1,3,256,128]{3,0,2,1:T(2,128)(2,1)S(1)} collective-permute-done((bf16[1,3,256,128]{3,0,2,1:T(2,128)(2,1)S(1)}, bf16[1,3,256,128]{3,0,2,1:T(2,128)(2,1)S(1)}, u32[]{:S(2)}, u32[]{:S(2)}) %collective-permute-start.2) | collective-permute-done | bytes 196640 | tf_op jit(solution)/shard_map/ppermute | solution.py:35
  57.4 5.5 copy.64
  62.9 41.8 %pad_maximum_fusion = bf16[1,70,262,128]{3,0,2,1:T(2,128)(2,1)S(1)} fusion(bf16[1,70,3,128]{3,0,2,1:T(2,128)(2,1)S(1)} %collective-permute-done.5, bf16[1,3,256,128]{3,0,2,1:T(2,128)(2,1)S(1)} %broadcast_select_fusion.4, bf16[1,64,256,128]{3,0,2,1:T(2,128)(2,1)} %copy-done, bf16[1,3,256,128]{3,0,2,1:T(2,128)(2,1)S(1)} %collective-permute-done, ...), kind=kLoop, calls=%fused_computation.47 | loop fusion | flops 9390080 | bytes 9390080 | tf_op jit(solution)/shard_map/concatenate | solution.py:24
  110.8 34.0 %select_add_fusion.1 = f32[64,8,33,128]{3,1,2,0:T(8,128)S(1)} fusion(f32[128]{0:T(128)S(1)} %copy-done.20, pred[8,33]{0,1:T(8,128)(4,1)S(1)} %copy-done.21, bf16[70,1,7,6,128]{4,2,3,0,1:T(8,128)(2,1)S(1)} %slice.80, bf16[70,1,8,33,128]{4,2,3,0,1:T(8,128)(2,1)S(1)} %copy.59, bf16[7,7,1,128]{3,1,0,2:T(8,128)(2,1)S(1)} %bitcast.144), kind=kOutput, calls=%fused_computation.48 | convolution fusion | flops 233041920 | bytes 14147592 | tf_op jit(solution)/shard_map/conv_general_dilated | solution.py:53
  148.2 4.9 copy.62
  153.1 4.2 copy.63
  157.3 98.5 %while.22 = (s32[]{:T(128)}, f32[128,256]{1,0:T(8,128)S(1)}, f32[256]{0:T(256)S(1)}, f32[256,128]{1,0:T(8,128)S(1)}, f32[128]{0:T(128)S(1)}, /*index=5*/f32[128]...) while((s32[]{:T(128)}, f32[128,256]{1,0:T(8,128)S(1)}, ...), condition=%wide.region_8.9_spmd.clone, body=%wide.region_0.8_spmd.clone.sunk | while | flops 1393168896 | bytes 81850672 | solution.py:141
  163.2 3.9 convolution_add_fusion.4
  169.8 3.9 fusion.103
  178.1 4.1 fusion.106
  187.7 3.9 convolution_add_fusion.4
  194.3 3.9 fusion.103
  202.6 4.1 fusion.106
  212.2 3.9 convolution_add_fusion.4
  218.8 3.9 fusion.103
  227.1 4.1 fusion.106
  236.7 3.9 convolution_add_fusion.4
  243.3 3.9 fusion.103
  251.6 4.1 fusion.106
  255.8 4.5 convert_reduce_fusion
  265.4 90.3 %fusion.29 = f32[1,7,7,128]{3,0,2,1:T(1,128)S(1)} fusion(bf16[1,70,262,128]{3,0,2,1:T(2,128)(2,1)} %copy-done.3, bf16[64,256,1,128]{3,1,0,2:T(8,128)(2,1)S(1)} %bitcast.128), kind=kOutput, calls=%fused_computation.51 | convolution fusion | flops 205520896 | bytes 8914432 | tf_op jit(solution)/shard_map/conv_general_dilated | solution.py:65
  355.8 57.7 %all-reduce = (f32[7,7,128]{2,1,0:T(8,128)S(1)}, f32[128]{0:T(128)S(1)}, f32[128]{0:T(128)S(1)}, f32[128]{0:T(128)S(1)}, f32[256]{0:T(256)S(1)}) all-reduce(f32[7,7,128]{2,1,0:T(8,128)S(1)} %bitcast.143, f32[128]{0:T(128)S(1)} %convert_reduce_fusion, ...), channel_id=1, replica_groups=mesh['groups'=2,'lon'=4,'lat'=2,'dp'=2] {'lon','lat','dp'}, use_global_device_ids=true, to_apply=%region_11.12 | all-reduce | flops 6912 | bytes 55296 | tf_op jit(solution)/shard_map/psum | solution.py:175
  417.3 91.0 %all-reduce.4.cloned.1.call-done = (f32[128,256]{1,0:T(8,128)}, f32[256,128]{1,0:T(8,128)}) async-done(((f32[128,256]{1,0:T(8,128)}, f32[256,128]{1,0:T(8,128)}), (f32[128,256]{1,0:T(8,128)}, f32[256,128]{1,0:T(8,128)})) %all-reduce.4.cloned.1.call-update) | async-done | bytes 262160 | tf_op jit(solution)/shard_map/psum | solution.py:175
  519.2 5.8 pad_maximum_fusion.1
  534.1 33.5 %broadcast_select_fusion.2 = f32[64,8,33,128]{3,1,2,0:T(8,128)S(1)} fusion(pred[8,33]{0,1:T(8,128)(4,1)S(1)} %copy-done.22, bf16[70,1,7,6,128]{4,2,3,0,1:T(8,128)(2,1)S(1)} %slice.85, bf16[70,1,8,33,128]{4,2,3,0,1:T(8,128)(2,1)S(1)} %copy.72, bf16[7,7,1,128]{3,1,0,2:T(8,128)(2,1)S(1)} %bitcast.146), kind=kOutput, calls=%fused_computation.69 | convolution fusion | flops 230879232 | bytes 14147080 | tf_op jit(solution)/shard_map/conv_general_dilated | solution.py:53
  567.7 4.9 copy.74
  572.6 6.2 %fusion.28 = f32[1,64,256,128]{3,1,2,0:T(8,128)S(1)} fusion(f32[64,1,264,128]{3,0,2,1:T(8,128)} %bitcast.133, bf16[1,64,256,128]{3,2,1,0:T(8,128)(2,1)S(1)} %copy-done.5), kind=kLoop, calls=%fused_computation.50 | loop fusion | flops 4194304 | bytes 20971520 | tf_op jit(solution)/shard_map/add | solution.py:165
  582.2 7.6 %scatter-add.4 = f32[1,64,256,128]{3,1,2,0:T(8,128)} dynamic-update-slice(f32[1,64,256,128]{3,1,2,0:T(8,128)} %copy-done.4, f32[1,3,256,128]{3,1,2,0:T(4,128)S(1)} %fusion.51, s32[]{:T(128)} %constant.89.clone.1, s32[]{:T(128)} %constant.94.clone.1, s32[]{:T(128)} %constant.89.clone.1, s32[]{:T(128)} %constant.89.clone.1) | dynamic-update-slice | bytes 786436 | tf_op jit(solution)/shard_map/scatter-add | solution.py:166
  589.8 4.5 convert_element_type.43
  594.3 4.7 copy.82
  (188 shorter events, 112.2 us)
Async XLA Ops:
  7.2 501.1 %all-reduce.4.cloned.1.call-start = ((), (), s32[]{:S(2)}) async-start(), calls=%async_computation | async-start | bytes 524288 | tf_op jit(solution)/shard_map/psum | solution.py:175
  19.1 12.2 %collective-permute-start.1 = (bf16[1,3,256,128]{3,0,2,1:T(2,128)(2,1)S(1)}, bf16[1,3,256,128]{3,0,2,1:T(2,128)(2,1)S(1)}, u32[]{:S(2)}, u32[]{:S(2)}) collective-permute-start(bf16[1,3,256,128]{3,0,2,1:T(2,128)(2,1)S(1)} %get-tuple-element.224), channel_id=1, source_target_pairs={{0,4},{4,0},{8,12},{12,8},{1,5},{5,1},{9,13},{13,9},{2,6},{6,2},{1... | collective-permute-start | bytes 589832 | tf_op jit(solution)/shard_map/ppermute | solution.py:35
  22.1 15.3 %collective-permute-start.3 = (bf16[1,3,256,128]{3,0,2,1:T(2,128)(2,1)S(1)}, bf16[1,3,256,128]{3,0,2,1:T(2,128)(2,1)S(1)}, u32[]{:S(2)}, u32[]{:S(2)}) collective-permute-start(bf16[1,3,256,128]{3,0,2,1:T(2,128)(2,1)S(1)} %get-tuple-element.225), channel_id=1, source_target_pairs={{2,0},{3,1},{6,4},{7,5},{10,8},{11,9},{14,12},{15,13},{18,16},{19,... | collective-permute-start | bytes 589832 | tf_op jit(solution)/shard_map/ppermute | solution.py:23
  31.3 19.6 %collective-permute-start.2 = (bf16[1,3,256,128]{3,0,2,1:T(2,128)(2,1)S(1)}, bf16[1,3,256,128]{3,0,2,1:T(2,128)(2,1)S(1)}, u32[]{:S(2)}, u32[]{:S(2)}) collective-permute-start(bf16[1,3,256,128]{3,0,2,1:T(2,128)(2,1)S(1)} %collective-permute-done.1), channel_id=1, source_target_pairs={{0,8},{8,0},{4,12},{12,4},{1,9},{9,1},{5,13},{13,5},{2,10},{10,2},... | collective-permute-start | bytes 589832 | tf_op jit(solution)/shard_map/ppermute | solution.py:35
  34.0 17.5 %collective-permute-start = (bf16[1,3,256,128]{3,0,2,1:T(2,128)(2,1)S(1)}, bf16[1,3,256,128]{3,0,2,1:T(2,128)(2,1)S(1)}, u32[]{:S(2)}, u32[]{:S(2)}) collective-permute-start(bf16[1,3,256,128]{3,0,2,1:T(2,128)(2,1)S(1)} %get-tuple-element.224), channel_id=1, source_target_pairs={{0,2},{1,3},{4,6},{5,7},{8,10},{9,11},{12,14},{13,15},{16,18},{17,... | collective-permute-start | bytes 589832 | tf_op jit(solution)/shard_map/ppermute | solution.py:20
  51.5 5.2 copy-start.19
  51.5 5.2 copy-start.15
  52.8 10.1 %collective-permute-start.4 = (bf16[1,70,3,128]{3,0,2,1:T(2,128)(2,1)S(1)}, bf16[1,70,3,128]{3,0,2,1:T(2,128)(2,1)S(1)}, u32[]{:S(2)}, u32[]{:S(2)}) collective-permute-start(bf16[1,70,3,128]{3,0,2,1:T(2,128)(2,1)S(1)} %get-tuple-element.222), channel_id=1, source_target_pairs={{0,4},{4,8},{8,12},{12,0},{1,5},{5,9},{9,13},{13,1},{2,6},{6,10},{... | collective-permute-start | bytes 161288 | tf_op jit(solution)/shard_map/ppermute | solution.py:20
  53.4 9.5 %collective-permute-start.5 = (bf16[1,70,3,128]{3,0,2,1:T(2,128)(2,1)S(1)}, bf16[1,70,3,128]{3,0,2,1:T(2,128)(2,1)S(1)}, u32[]{:S(2)}, u32[]{:S(2)}) collective-permute-start(bf16[1,70,3,128]{3,0,2,1:T(2,128)(2,1)S(1)} %get-tuple-element.223), channel_id=1, source_target_pairs={{4,0},{8,4},{12,8},{0,12},{5,1},{9,5},{13,9},{1,13},{6,2},{10,6},{... | collective-permute-start | bytes 161288 | tf_op jit(solution)/shard_map/ppermute | solution.py:23
  153.1 4.2 copy-start.9
  153.1 4.2 copy-start.11
  160.5 6.6 %copy-start.8 = (bf16[4,4096,128]{2,1,0:T(8,128)(2,1)S(1)}, bf16[4,4096,128]{2,1,0:T(8,128)(2,1)}, u32[]{:S(2)}) copy-start(bf16[4,4096,128]{2,1,0:T(8,128)(2,1)} %get-tuple-element.391) | copy-start | bytes 12582916 | tf_op jit(solution)/shard_map/while
  167.1 6.6 %slice-start = ((s8[8388608]{0:T(1024)(128)(4,1)}), s8[4194304]{0:T(1024)(128)(4,1)S(1)}, s32[]{:S(2)}) async-start(s8[8388608]{0:T(1024)(128)(4,1)} %bitcast.125), calls=%async_computation.1 | async-start | bytes 8388608 | tf_op jit(solution)/shard_map/while
  185.0 6.6 %copy-start.8 = (bf16[4,4096,128]{2,1,0:T(8,128)(2,1)S(1)}, bf16[4,4096,128]{2,1,0:T(8,128)(2,1)}, u32[]{:S(2)}) copy-start(bf16[4,4096,128]{2,1,0:T(8,128)(2,1)} %get-tuple-element.391) | copy-start | bytes 12582916 | tf_op jit(solution)/shard_map/while
  191.6 6.6 %slice-start = ((s8[8388608]{0:T(1024)(128)(4,1)}), s8[4194304]{0:T(1024)(128)(4,1)S(1)}, s32[]{:S(2)}) async-start(s8[8388608]{0:T(1024)(128)(4,1)} %bitcast.125), calls=%async_computation.1 | async-start | bytes 8388608 | tf_op jit(solution)/shard_map/while
  209.5 6.6 %copy-start.8 = (bf16[4,4096,128]{2,1,0:T(8,128)(2,1)S(1)}, bf16[4,4096,128]{2,1,0:T(8,128)(2,1)}, u32[]{:S(2)}) copy-start(bf16[4,4096,128]{2,1,0:T(8,128)(2,1)} %get-tuple-element.391) | copy-start | bytes 12582916 | tf_op jit(solution)/shard_map/while
  216.2 6.6 %slice-start = ((s8[8388608]{0:T(1024)(128)(4,1)}), s8[4194304]{0:T(1024)(128)(4,1)S(1)}, s32[]{:S(2)}) async-start(s8[8388608]{0:T(1024)(128)(4,1)} %bitcast.125), calls=%async_computation.1 | async-start | bytes 8388608 | tf_op jit(solution)/shard_map/while
  234.1 6.6 %copy-start.8 = (bf16[4,4096,128]{2,1,0:T(8,128)(2,1)S(1)}, bf16[4,4096,128]{2,1,0:T(8,128)(2,1)}, u32[]{:S(2)}) copy-start(bf16[4,4096,128]{2,1,0:T(8,128)(2,1)} %get-tuple-element.391) | copy-start | bytes 12582916 | tf_op jit(solution)/shard_map/while
  240.7 6.6 %slice-start = ((s8[8388608]{0:T(1024)(128)(4,1)}), s8[4194304]{0:T(1024)(128)(4,1)S(1)}, s32[]{:S(2)}) async-start(s8[8388608]{0:T(1024)(128)(4,1)} %bitcast.125), calls=%async_computation.1 | async-start | bytes 8388608 | tf_op jit(solution)/shard_map/while
  255.8 5.9 copy-start.7
  255.8 5.9 copy-start.10
  255.8 4.5 copy-start.6
  261.7 94.0 %copy-start.1 = (bf16[1,64,4,64,128]{4,3,2,1,0:T(8,128)(2,1)}, bf16[1,64,4,64,128]{4,3,2,1,0:T(8,128)(2,1)S(1)}, u32[]{:S(2)}) copy-start(bf16[1,64,4,64,128]{4,3,2,1,0:T(8,128)(2,1)S(1)} %copy.65) | copy-start | bytes 12582916
  262.1 154.7 %collective-permute-start.7 = (bf16[1,3,256,128]{3,0,2,1:T(2,128)(2,1)S(1)}, bf16[1,3,256,128]{3,0,2,1:T(2,128)(2,1)S(1)}, u32[]{:S(2)}, u32[]{:S(2)}) collective-permute-start(bf16[1,3,256,128]{3,0,2,1:T(2,128)(2,1)S(1)} %copy.87), channel_id=1, source_target_pairs={{0,4},{4,0},{8,12},{12,8},{1,5},{5,1},{9,13},{13,9},{2,6},{6,2},{1... | collective-permute-start | bytes 589832 | tf_op jit(solution)/shard_map/ppermute | solution.py:35
  262.1 247.8 %collective-permute-start.6 = (bf16[1,3,256,128]{3,0,2,1:T(2,128)(2,1)S(1)}, bf16[1,3,256,128]{3,0,2,1:T(2,128)(2,1)S(1)}, u32[]{:S(2)}, u32[]{:S(2)}) collective-permute-start(bf16[1,3,256,128]{3,0,2,1:T(2,128)(2,1)S(1)} %copy.87), channel_id=1, source_target_pairs={{0,2},{1,3},{4,6},{5,7},{8,10},{9,11},{12,14},{13,15},{16,18},{17,... | collective-permute-start | bytes 589832 | tf_op jit(solution)/shard_map/ppermute | solution.py:20
  414.9 95.1 %collective-permute-start.9 = (bf16[1,3,256,128]{3,0,2,1:T(2,128)(2,1)S(1)}, bf16[1,3,256,128]{3,0,2,1:T(2,128)(2,1)S(1)}, u32[]{:S(2)}, u32[]{:S(2)}) collective-permute-start(bf16[1,3,256,128]{3,0,2,1:T(2,128)(2,1)S(1)} %copy.88), channel_id=1, source_target_pairs={{2,0},{3,1},{6,4},{7,5},{10,8},{11,9},{14,12},{15,13},{18,16},{19,... | collective-permute-start | bytes 589832 | tf_op jit(solution)/shard_map/ppermute | solution.py:23
  416.7 93.2 %collective-permute-start.8 = (bf16[1,3,256,128]{3,0,2,1:T(2,128)(2,1)S(1)}, bf16[1,3,256,128]{3,0,2,1:T(2,128)(2,1)S(1)}, u32[]{:S(2)}, u32[]{:S(2)}) collective-permute-start(bf16[1,3,256,128]{3,0,2,1:T(2,128)(2,1)S(1)} %collective-permute-done.7), channel_id=1, source_target_pairs={{0,8},{8,0},{4,12},{12,4},{1,9},{9,1},{5,13},{13,5},{2,10},{10,2},... | collective-permute-start | bytes 589832 | tf_op jit(solution)/shard_map/ppermute | solution.py:35
  508.3 7.3 %copy-start.13 = (f32[256,128]{1,0:T(8,128)S(1)}, f32[256,128]{1,0:T(8,128)}, u32[]{:S(2)}) copy-start(f32[256,128]{1,0:T(8,128)} %get-tuple-element.212) | copy-start | bytes 393220
  508.3 10.9 %copy-start.2 = (bf16[1,64,4,64,128]{4,3,2,1,0:T(8,128)(2,1)S(1)}, bf16[1,64,4,64,128]{4,3,2,1,0:T(8,128)(2,1)}, u32[]{:S(2)}) copy-start(bf16[1,64,4,64,128]{4,3,2,1,0:T(8,128)(2,1)} %copy-done.1) | copy-start | bytes 12582916
  511.7 6.9 %collective-permute-start.10 = (bf16[1,70,3,128]{3,2,1,0:T(4,128)(2,1)S(1)}, bf16[1,70,3,128]{3,2,1,0:T(4,128)(2,1)S(1)}, u32[]{:S(2)}, u32[]{:S(2)}) collective-permute-start(bf16[1,70,3,128]{3,2,1,0:T(4,128)(2,1)S(1)} %get-tuple-element.226), channel_id=1, source_target_pairs={{0,4},{4,8},{8,12},{12,0},{1,5},{5,9},{9,13},{13,1},{2,6},{6,10},{... | collective-permute-start | bytes 161288 | tf_op jit(solution)/shard_map/ppermute | solution.py:20
  514.7 4.5 collective-permute-start.11
  567.7 4.9 copy-start.5
  (15 other events, 42.8 us)
Sparse Core Ops, SparseCore 0:
  416.3 91.9 all-reduce.3
where the time goes:
time: 611 us; the launch traced here: 606 us
  matrix products  218 us (36%)
  waiting for transfers between devices  115 us (19%)
  other arithmetic  110 us (18%)
  local copies, waits for them, and re-layouts  66.8 us (11%)
  blocking collectives  57.7 us (9%)
  starting transfers between devices  23 us (4%)
  between operations  14.9 us (2%)
    psum x1, waiting for transfers between devices, local(): lax.psum((g_in, g_out, g_kernel, g_bias, g_gain, g_shift, g_bin), ('lon',...  91 us
    conv_general_dilated x1, matrix products, kernel_grad(): lax.conv_general_dilated(extended[None], delta[:, :, None, :], (1, 1), 'V...  90.3 us
    conv_general_dilated x3, matrix products, conv_valid(): lax.conv_general_dilated(extended, kernel[:, :, None, :], (1, 1), 'VALID'...  68.3 us
    psum x1, blocking collectives, local(): lax.psum((g_in, g_out, g_kernel, g_bias, g_gain, g_shift, g_bin), ('lon',...  57.7 us
    concatenate x2, other arithmetic, padded(): block = jnp.concatenate([low, block, high], axis=dim)  47.6 us
    unnamed x52, local copies, waits for them, and re-layouts  25.1 us
    ppermute x4, waiting for transfers between devices, partner(): return lax.ppermute(block, axis, route)  21.3 us
    dynamic_update_slice x4, other arithmetic, local(): lax.scan(step, totals, (to_blocks(field_y), to_blocks(cotangent), masks))  16.5 us
  transfers between devices with their start and end apart: 13, of which 5 were waited for; matrix products, arithmetic and copies ran while one was open for 17% of the time, Pallas kernels for 0%

commit v1 on v0

--- a/solution.py
+++ b/solution.py
@@ -172,7 +172,8 @@
     scale = 1.0 / math.sqrt(cells_all)
     in_share = chans // lax.axis_size("dp")
     out_share = hidden // lax.axis_size("dp")
-    summed = lax.psum((g_in, g_out, g_kernel, g_bias, g_gain, g_shift, g_bin), ("lon", "lat", "dp"))
+    partial = lax.psum((g_in, g_out, g_kernel, g_bias, g_gain, g_shift, g_bin), ("lat", "dp"))
+    summed = lax.psum(partial, "lon")
     s_in, s_out, s_kernel, s_bias, s_gain, s_shift, s_bin = summed
     position = lax.axis_index("dp")
     s_in = lax.dynamic_slice_in_dim(s_in, position * in_share, in_share, 0)

time: 611 us -> 554 us (0.907)
  waiting for transfers between devices: 115 us -> 83.7 us
  blocking collectives: 57.7 us -> 28 us
    psum x1 -> x2, blocking collectives: 57.7 us -> 28 us  [the longest x1 17.7 us: local(): summed = lax.psum(partial, 'lon')]
    psum x1 -> x2, waiting for transfers between devices: 91 us -> 62.4 us  [the longest x1 32.4 us: local(): summed = lax.psum(partial, 'lon')]
    unnamed x52 -> x50, local copies, waits for them, and re-layouts: 25.1 us -> 26.3 us
  transfers between devices with their start and end apart: 13 -> 14, of which waited for: 5 -> 4; matrix products, arithmetic and copies ran while one was open for 17% -> 19% of each run, Pallas kernels for 0% -> 0%
where the time goes in v1:
time: 554 us; the launch traced here: 549 us
  matrix products  218 us (39%)
  other arithmetic  112 us (20%)
  waiting for transfers between devices  83.7 us (15%)
  local copies, waits for them, and re-layouts  68.2 us (12%)
  blocking collectives  28 us (5%)
  starting transfers between devices  23.6 us (4%)
  between operations  14.9 us (3%)
    conv_general_dilated x1, matrix products, kernel_grad(): lax.conv_general_dilated(extended[None], delta[:, :, None, :], (1, 1), 'V...  90.3 us
    conv_general_dilated x3, matrix products, conv_valid(): lax.conv_general_dilated(extended, kernel[:, :, None, :], (1, 1), 'VALID'...  68.3 us
    concatenate x2, other arithmetic, padded(): block = jnp.concatenate([low, block, high], axis=dim)  49.1 us
    psum x1, waiting for transfers between devices, local(): summed = lax.psum(partial, 'lon')  32.4 us
    psum x1, waiting for transfers between devices, local(): lax.psum((g_in, g_out, g_kernel, g_bias, g_gain, g_shift, g_bin), ('lat',...  30 us
    unnamed x50, local copies, waits for them, and re-layouts  26.3 us
    ppermute x4, waiting for transfers between devices, partner(): return lax.ppermute(block, axis, route)  21.3 us
    psum x1, blocking collectives, local(): summed = lax.psum(partial, 'lon')  17.7 us
  transfers between devices with their start and end apart: 14, of which 4 were waited for; matrix products, arithmetic and copies ran while one was open for 19% of the time, Pallas kernels for 0%

profile of v1, /device:TPU:0, one launch (start us, length us, event | category | flops | bytes accessed | tf_op | source)
XLA Modules:
  0.0 549.2 jit_solution(4856750972362839399)
XLA Ops:
  7.2 7.8 %copy.54 = bf16[1,64,256,128]{3,0,2,1:T(2,128)(2,1)S(1)} copy(bf16[1,64,256,128]{3,2,1,0:T(8,128)(2,1)} %param.14) | data formatting | bytes 8388608 | tf_op args[0]
  23.4 7.8 %collective-permute-done.1 = bf16[1,3,256,128]{3,0,2,1:T(2,128)(2,1)S(1)} collective-permute-done((bf16[1,3,256,128]{3,0,2,1:T(2,128)(2,1)S(1)}, bf16[1,3,256,128]{3,0,2,1:T(2,128)(2,1)S(1)}, u32[]{:S(2)}, u32[]{:S(2)}) %collective-permute-start.1) | collective-permute-done | bytes 196640 | tf_op jit(solution)/shard_map/ppermute | solution.py:35
  37.4 13.4 %collective-permute-done.2 = bf16[1,3,256,128]{3,0,2,1:T(2,128)(2,1)S(1)} collective-permute-done((bf16[1,3,256,128]{3,0,2,1:T(2,128)(2,1)S(1)}, bf16[1,3,256,128]{3,0,2,1:T(2,128)(2,1)S(1)}, u32[]{:S(2)}, u32[]{:S(2)}) %collective-permute-start.2) | collective-permute-done | bytes 196640 | tf_op jit(solution)/shard_map/ppermute | solution.py:35
  57.4 5.5 %copy.64 = bf16[1,64,4,64,128]{4,3,1,2,0:T(8,128)(2,1)} copy(bf16[1,64,4,64,128]{4,3,2,1,0:T(8,128)(2,1)} %bitcast.138) | data formatting | bytes 8388608 | tf_op jit(solution)/shard_map/reshape | solution.py:124
  62.9 41.8 %pad_maximum_fusion = bf16[1,70,262,128]{3,0,2,1:T(2,128)(2,1)S(1)} fusion(bf16[1,70,3,128]{3,0,2,1:T(2,128)(2,1)S(1)} %collective-permute-done.5, bf16[1,3,256,128]{3,0,2,1:T(2,128)(2,1)S(1)} %broadcast_select_fusion.4, bf16[1,64,256,128]{3,0,2,1:T(2,128)(2,1)} %copy-done, bf16[1,3,256,128]{3,0,2,1:T(2,128)(2,1)S(1)} %collective-permute-done, ...), kind=kLoop, calls=%fused_computation.47 | loop fusion | flops 9390080 | bytes 9390080 | tf_op jit(solution)/shard_map/concatenate | solution.py:24
  110.8 34.0 %select_add_fusion.1 = f32[64,8,33,128]{3,1,2,0:T(8,128)S(1)} fusion(f32[128]{0:T(128)S(1)} %copy-done.19, pred[8,33]{0,1:T(8,128)(4,1)S(1)} %copy-done.20, bf16[70,1,7,6,128]{4,2,3,0,1:T(8,128)(2,1)S(1)} %slice.80, bf16[70,1,8,33,128]{4,2,3,0,1:T(8,128)(2,1)S(1)} %copy.59, bf16[7,7,1,128]{3,1,0,2:T(8,128)(2,1)S(1)} %bitcast.144), kind=kOutput, calls=%fused_computation.48 | convolution fusion | flops 233041920 | bytes 14147592 | tf_op jit(solution)/shard_map/conv_general_dilated | solution.py:53
  148.2 4.9 copy.62
  153.1 4.2 copy.63
  157.3 98.5 %while.22 = (s32[]{:T(128)}, f32[128,256]{1,0:T(8,128)S(1)}, f32[256]{0:T(256)S(1)}, f32[256,128]{1,0:T(8,128)S(1)}, f32[128]{0:T(128)S(1)}, /*index=5*/f32[128]...) while((s32[]{:T(128)}, f32[128,256]{1,0:T(8,128)S(1)}, ...), condition=%wide.region_8.9_spmd.clone, body=%wide.region_0.8_spmd.clone.sunk | while | flops 1393168896 | bytes 81850672 | solution.py:141
  163.2 3.9 convolution_add_fusion.4
  169.8 3.9 fusion.103
  178.1 4.1 fusion.106
  194.3 3.9 fusion.103
  202.6 4.1 fusion.106
  212.2 3.9 convolution_add_fusion.4
  218.8 3.9 fusion.103
  227.1 4.1 fusion.106
  243.3 3.9 fusion.103
  251.6 4.1 fusion.106
  255.7 4.5 convert_reduce_fusion
  265.4 90.3 %fusion.29 = f32[1,7,7,128]{3,0,2,1:T(1,128)S(1)} fusion(bf16[1,70,262,128]{3,0,2,1:T(2,128)(2,1)} %copy-done.3, bf16[64,256,1,128]{3,1,0,2:T(8,128)(2,1)S(1)} %bitcast.128), kind=kOutput, calls=%fused_computation.51 | convolution fusion | flops 205520896 | bytes 8914432 | tf_op jit(solution)/shard_map/conv_general_dilated | solution.py:65
  355.7 10.3 %all-reduce = (f32[7,7,128]{2,1,0:T(8,128)S(1)}, f32[128]{0:T(128)S(1)}, f32[128]{0:T(128)S(1)}, f32[128]{0:T(128)S(1)}, f32[256]{0:T(256)S(1)}) all-reduce(f32[7,7,128]{2,1,0:T(8,128)S(1)} %bitcast.143, f32[128]{0:T(128)S(1)} %convert_reduce_fusion, ...), channel_id=1, replica_groups=mesh['groups'=2,'lon'=4,'lat'=2,'dp'=2] {'lat','dp'}, use_global_device_ids=true, to_apply=%region_13.14 | all-reduce | flops 6912 | bytes 55296 | tf_op jit(solution)/shard_map/psum | solution.py:175
  366.0 17.7 %all-reduce.2 = (f32[7,7,128]{2,1,0:T(8,128)S(1)}, f32[128]{0:T(128)S(1)}, f32[128]{0:T(128)S(1)}, f32[128]{0:T(128)S(1)}, f32[256]{0:T(256)S(1)}) all-reduce(f32[7,7,128]{2,1,0:T(8,128)S(1)} %get-tuple-element.206, f32[128]{0:T(128)S(1)} %get-tuple-element.207, ...), channel_id=1, replica_groups=mesh['groups'=2,'lon'=4,'lat'=2,'dp'=2] {'lon'}, use_global_device_ids=true, to_apply=%region_14.15 | all-reduce | flops 6912 | bytes 55296 | tf_op jit(solution)/shard_map/psum | solution.py:176
  388.3 30.0 %all-reduce.7.cloned.1.call-done = (f32[128,256]{1,0:T(8,128)}, f32[256,128]{1,0:T(8,128)}) async-done(((f32[128,256]{1,0:T(8,128)}, f32[256,128]{1,0:T(8,128)}), (f32[128,256]{1,0:T(8,128)}, f32[256,128]{1,0:T(8,128)})) %all-reduce.7.cloned.1.call-update) | async-done | bytes 262160 | tf_op jit(solution)/shard_map/psum | solution.py:175
  423.9 32.4 %all-reduce.9.cloned.1.call-done = (f32[128,256]{1,0:T(8,128)}, f32[256,128]{1,0:T(8,128)}) async-done(((f32[128,256]{1,0:T(8,128)}, f32[256,128]{1,0:T(8,128)}), (f32[128,256]{1,0:T(8,128)}, f32[256,128]{1,0:T(8,128)})) %all-reduce.9.cloned.1.call-update) | async-done | bytes 262160 | tf_op jit(solution)/shard_map/psum | solution.py:176
  459.3 7.3 %pad_maximum_fusion.1 = bf16[1,70,262,128]{3,2,1,0:T(8,128)(2,1)S(1)} fusion(bf16[1,70,3,128]{3,2,1,0:T(4,128)(2,1)S(1)} %collective-permute-done.11, bf16[1,3,256,128]{3,2,1,0:T(8,128)(2,1)S(1)} %copy.69, bf16[1,64,256,128]{3,2,1,0:T(8,128)(2,1)} %bitcast.130, bf16[1,3,256,128]{3,2,1,0:T(8,128)(2,1)S(1)} %copy.68, ...), kind=kLoop, calls=%fused_computation.66 | loop fusion | flops 23475200 | bytes 9390080 | tf_op jit(solution)/shard_map/concatenate | solution.py:24
  477.2 33.5 %broadcast_select_fusion.2 = f32[64,8,33,128]{3,1,2,0:T(8,128)S(1)} fusion(pred[8,33]{0,1:T(8,128)(4,1)S(1)} %copy-done.21, bf16[70,1,7,6,128]{4,2,3,0,1:T(8,128)(2,1)S(1)} %slice.85, bf16[70,1,8,33,128]{4,2,3,0,1:T(8,128)(2,1)S(1)} %copy.72, bf16[7,7,1,128]{3,1,0,2:T(8,128)(2,1)S(1)} %bitcast.146), kind=kOutput, calls=%fused_computation.69 | convolution fusion | flops 230879232 | bytes 14147080 | tf_op jit(solution)/shard_map/conv_general_dilated | solution.py:53
  510.7 4.9 copy.74
  515.7 6.2 %fusion.28 = f32[1,64,256,128]{3,1,2,0:T(8,128)S(1)} fusion(f32[64,1,264,128]{3,0,2,1:T(8,128)} %bitcast.133, bf16[1,64,256,128]{3,2,1,0:T(8,128)(2,1)S(1)} %copy-done.5), kind=kLoop, calls=%fused_computation.50 | loop fusion | flops 4194304 | bytes 20971520 | tf_op jit(solution)/shard_map/add | solution.py:165
  525.3 7.6 %scatter-add.4 = f32[1,64,256,128]{3,1,2,0:T(8,128)} dynamic-update-slice(f32[1,64,256,128]{3,1,2,0:T(8,128)} %copy-done.4, f32[1,3,256,128]{3,1,2,0:T(4,128)S(1)} %fusion.51, s32[]{:T(128)} %constant.89.clone.1, s32[]{:T(128)} %constant.94.clone.1, s32[]{:T(128)} %constant.89.clone.1, s32[]{:T(128)} %constant.89.clone.1) | dynamic-update-slice | bytes 786436 | tf_op jit(solution)/shard_map/scatter-add | solution.py:166
  532.9 4.5 convert_element_type.43
  537.4 4.7 copy.82
  (190 shorter events, 119.8 us)
Async XLA Ops:
  7.2 411.1 %all-reduce.7.cloned.1.call-start = ((), (), s32[]{:S(2)}) async-start(), calls=%async_computation | async-start | bytes 524288 | tf_op jit(solution)/shard_map/psum | solution.py:175
  19.0 12.2 %collective-permute-start.1 = (bf16[1,3,256,128]{3,0,2,1:T(2,128)(2,1)S(1)}, bf16[1,3,256,128]{3,0,2,1:T(2,128)(2,1)S(1)}, u32[]{:S(2)}, u32[]{:S(2)}) collective-permute-start(bf16[1,3,256,128]{3,0,2,1:T(2,128)(2,1)S(1)} %get-tuple-element.231), channel_id=1, source_target_pairs={{0,4},{4,0},{8,12},{12,8},{1,5},{5,1},{9,13},{13,9},{2,6},{6,2},{1... | collective-permute-start | bytes 589832 | tf_op jit(solution)/shard_map/ppermute | solution.py:35
  22.1 15.3 %collective-permute-start.3 = (bf16[1,3,256,128]{3,0,2,1:T(2,128)(2,1)S(1)}, bf16[1,3,256,128]{3,0,2,1:T(2,128)(2,1)S(1)}, u32[]{:S(2)}, u32[]{:S(2)}) collective-permute-start(bf16[1,3,256,128]{3,0,2,1:T(2,128)(2,1)S(1)} %get-tuple-element.232), channel_id=1, source_target_pairs={{2,0},{3,1},{6,4},{7,5},{10,8},{11,9},{14,12},{15,13},{18,16},{19,... | collective-permute-start | bytes 589832 | tf_op jit(solution)/shard_map/ppermute | solution.py:23
  31.3 19.6 %collective-permute-start.2 = (bf16[1,3,256,128]{3,0,2,1:T(2,128)(2,1)S(1)}, bf16[1,3,256,128]{3,0,2,1:T(2,128)(2,1)S(1)}, u32[]{:S(2)}, u32[]{:S(2)}) collective-permute-start(bf16[1,3,256,128]{3,0,2,1:T(2,128)(2,1)S(1)} %collective-permute-done.1), channel_id=1, source_target_pairs={{0,8},{8,0},{4,12},{12,4},{1,9},{9,1},{5,13},{13,5},{2,10},{10,2},... | collective-permute-start | bytes 589832 | tf_op jit(solution)/shard_map/ppermute | solution.py:35
  34.0 17.5 %collective-permute-start = (bf16[1,3,256,128]{3,0,2,1:T(2,128)(2,1)S(1)}, bf16[1,3,256,128]{3,0,2,1:T(2,128)(2,1)S(1)}, u32[]{:S(2)}, u32[]{:S(2)}) collective-permute-start(bf16[1,3,256,128]{3,0,2,1:T(2,128)(2,1)S(1)} %get-tuple-element.231), channel_id=1, source_target_pairs={{0,2},{1,3},{4,6},{5,7},{8,10},{9,11},{12,14},{13,15},{16,18},{17,... | collective-permute-start | bytes 589832 | tf_op jit(solution)/shard_map/ppermute | solution.py:20
  51.5 5.2 copy-start.18
  51.5 5.2 copy-start.14
  52.8 10.1 %collective-permute-start.4 = (bf16[1,70,3,128]{3,0,2,1:T(2,128)(2,1)S(1)}, bf16[1,70,3,128]{3,0,2,1:T(2,128)(2,1)S(1)}, u32[]{:S(2)}, u32[]{:S(2)}) collective-permute-start(bf16[1,70,3,128]{3,0,2,1:T(2,128)(2,1)S(1)} %get-tuple-element.229), channel_id=1, source_target_pairs={{0,4},{4,8},{8,12},{12,0},{1,5},{5,9},{9,13},{13,1},{2,6},{6,10},{... | collective-permute-start | bytes 161288 | tf_op jit(solution)/shard_map/ppermute | solution.py:20
  53.4 9.5 %collective-permute-start.5 = (bf16[1,70,3,128]{3,0,2,1:T(2,128)(2,1)S(1)}, bf16[1,70,3,128]{3,0,2,1:T(2,128)(2,1)S(1)}, u32[]{:S(2)}, u32[]{:S(2)}) collective-permute-start(bf16[1,70,3,128]{3,0,2,1:T(2,128)(2,1)S(1)} %get-tuple-element.230), channel_id=1, source_target_pairs={{4,0},{8,4},{12,8},{0,12},{5,1},{9,5},{13,9},{1,13},{6,2},{10,6},{... | collective-permute-start | bytes 161288 | tf_op jit(solution)/shard_map/ppermute | solution.py:23
  153.0 4.2 copy-start.9
  153.0 4.2 copy-start.11
  153.1 4.2 copy-start.12
  160.5 6.6 %copy-start.8 = (bf16[4,4096,128]{2,1,0:T(8,128)(2,1)S(1)}, bf16[4,4096,128]{2,1,0:T(8,128)(2,1)}, u32[]{:S(2)}) copy-start(bf16[4,4096,128]{2,1,0:T(8,128)(2,1)} %get-tuple-element.398) | copy-start | bytes 12582916 | tf_op jit(solution)/shard_map/while
  167.1 6.6 %slice-start = ((s8[8388608]{0:T(1024)(128)(4,1)}), s8[4194304]{0:T(1024)(128)(4,1)S(1)}, s32[]{:S(2)}) async-start(s8[8388608]{0:T(1024)(128)(4,1)} %bitcast.125), calls=%async_computation.2 | async-start | bytes 8388608 | tf_op jit(solution)/shard_map/while
  185.0 6.6 %copy-start.8 = (bf16[4,4096,128]{2,1,0:T(8,128)(2,1)S(1)}, bf16[4,4096,128]{2,1,0:T(8,128)(2,1)}, u32[]{:S(2)}) copy-start(bf16[4,4096,128]{2,1,0:T(8,128)(2,1)} %get-tuple-element.398) | copy-start | bytes 12582916 | tf_op jit(solution)/shard_map/while
  191.6 6.6 %slice-start = ((s8[8388608]{0:T(1024)(128)(4,1)}), s8[4194304]{0:T(1024)(128)(4,1)S(1)}, s32[]{:S(2)}) async-start(s8[8388608]{0:T(1024)(128)(4,1)} %bitcast.125), calls=%async_computation.2 | async-start | bytes 8388608 | tf_op jit(solution)/shard_map/while
  209.5 6.6 %copy-start.8 = (bf16[4,4096,128]{2,1,0:T(8,128)(2,1)S(1)}, bf16[4,4096,128]{2,1,0:T(8,128)(2,1)}, u32[]{:S(2)}) copy-start(bf16[4,4096,128]{2,1,0:T(8,128)(2,1)} %get-tuple-element.398) | copy-start | bytes 12582916 | tf_op jit(solution)/shard_map/while
  216.1 6.6 %slice-start = ((s8[8388608]{0:T(1024)(128)(4,1)}), s8[4194304]{0:T(1024)(128)(4,1)S(1)}, s32[]{:S(2)}) async-start(s8[8388608]{0:T(1024)(128)(4,1)} %bitcast.125), calls=%async_computation.2 | async-start | bytes 8388608 | tf_op jit(solution)/shard_map/while
  234.0 6.6 %copy-start.8 = (bf16[4,4096,128]{2,1,0:T(8,128)(2,1)S(1)}, bf16[4,4096,128]{2,1,0:T(8,128)(2,1)}, u32[]{:S(2)}) copy-start(bf16[4,4096,128]{2,1,0:T(8,128)(2,1)} %get-tuple-element.398) | copy-start | bytes 12582916 | tf_op jit(solution)/shard_map/while
  240.6 6.6 %slice-start = ((s8[8388608]{0:T(1024)(128)(4,1)}), s8[4194304]{0:T(1024)(128)(4,1)S(1)}, s32[]{:S(2)}) async-start(s8[8388608]{0:T(1024)(128)(4,1)} %bitcast.125), calls=%async_computation.2 | async-start | bytes 8388608 | tf_op jit(solution)/shard_map/while
  255.7 5.9 %copy-start.7 = (f32[128,256]{1,0:T(8,128)}, f32[128,256]{1,0:T(8,128)S(1)}, u32[]{:S(2)}) copy-start(f32[128,256]{1,0:T(8,128)S(1)} %get-tuple-element.103) | copy-start | bytes 393220
  255.7 5.9 %copy-start.10 = (f32[256,128]{1,0:T(8,128)}, f32[256,128]{1,0:T(8,128)S(1)}, u32[]{:S(2)}) copy-start(f32[256,128]{1,0:T(8,128)S(1)} %get-tuple-element.104) | copy-start | bytes 393220
  255.7 4.5 copy-start.6
  261.7 94.0 %copy-start.1 = (bf16[1,64,4,64,128]{4,3,2,1,0:T(8,128)(2,1)}, bf16[1,64,4,64,128]{4,3,2,1,0:T(8,128)(2,1)S(1)}, u32[]{:S(2)}) copy-start(bf16[1,64,4,64,128]{4,3,2,1,0:T(8,128)(2,1)S(1)} %copy.65) | copy-start | bytes 12582916
  262.0 125.1 %collective-permute-start.7 = (bf16[1,3,256,128]{3,0,2,1:T(2,128)(2,1)S(1)}, bf16[1,3,256,128]{3,0,2,1:T(2,128)(2,1)S(1)}, u32[]{:S(2)}, u32[]{:S(2)}) collective-permute-start(bf16[1,3,256,128]{3,0,2,1:T(2,128)(2,1)S(1)} %copy.87), channel_id=1, source_target_pairs={{0,4},{4,0},{8,12},{12,8},{1,5},{5,1},{9,13},{13,9},{2,6},{6,2},{1... | collective-permute-start | bytes 589832 | tf_op jit(solution)/shard_map/ppermute | solution.py:35
  262.1 156.2 %collective-permute-start.6 = (bf16[1,3,256,128]{3,0,2,1:T(2,128)(2,1)S(1)}, bf16[1,3,256,128]{3,0,2,1:T(2,128)(2,1)S(1)}, u32[]{:S(2)}, u32[]{:S(2)}) collective-permute-start(bf16[1,3,256,128]{3,0,2,1:T(2,128)(2,1)S(1)} %copy.87), channel_id=1, source_target_pairs={{0,2},{1,3},{4,6},{5,7},{8,10},{9,11},{12,14},{13,15},{16,18},{17,... | collective-permute-start | bytes 589832 | tf_op jit(solution)/shard_map/ppermute | solution.py:20
  385.3 33.1 %collective-permute-start.9 = (bf16[1,3,256,128]{3,0,2,1:T(2,128)(2,1)S(1)}, bf16[1,3,256,128]{3,0,2,1:T(2,128)(2,1)S(1)}, u32[]{:S(2)}, u32[]{:S(2)}) collective-permute-start(bf16[1,3,256,128]{3,0,2,1:T(2,128)(2,1)S(1)} %copy.88), channel_id=1, source_target_pairs={{2,0},{3,1},{6,4},{7,5},{10,8},{11,9},{14,12},{15,13},{18,16},{19,... | collective-permute-start | bytes 589832 | tf_op jit(solution)/shard_map/ppermute | solution.py:23
  386.6 69.8 %all-reduce.9.cloned.1.call-start = ((), (), s32[]{:S(2)}) async-start(), calls=%async_computation.1 | async-start | bytes 524288 | tf_op jit(solution)/shard_map/psum | solution.py:176
  387.2 31.2 %collective-permute-start.8 = (bf16[1,3,256,128]{3,0,2,1:T(2,128)(2,1)S(1)}, bf16[1,3,256,128]{3,0,2,1:T(2,128)(2,1)S(1)}, u32[]{:S(2)}, u32[]{:S(2)}) collective-permute-start(bf16[1,3,256,128]{3,0,2,1:T(2,128)(2,1)S(1)} %collective-permute-done.7), channel_id=1, source_target_pairs={{0,8},{8,0},{4,12},{12,4},{1,9},{9,1},{5,13},{13,5},{2,10},{10,2},... | collective-permute-start | bytes 589832 | tf_op jit(solution)/shard_map/ppermute | solution.py:35
  420.0 39.3 %collective-permute-start.10 = (bf16[1,70,3,128]{3,2,1,0:T(4,128)(2,1)S(1)}, bf16[1,70,3,128]{3,2,1,0:T(4,128)(2,1)S(1)}, u32[]{:S(2)}, u32[]{:S(2)}) collective-permute-start(bf16[1,70,3,128]{3,2,1,0:T(4,128)(2,1)S(1)} %get-tuple-element.233), channel_id=1, source_target_pairs={{0,4},{4,8},{8,12},{12,0},{1,5},{5,9},{9,13},{13,1},{2,6},{6,10},{... | collective-permute-start | bytes 161288 | tf_op jit(solution)/shard_map/ppermute | solution.py:20
  421.6 37.7 %collective-permute-start.11 = (bf16[1,70,3,128]{3,2,1,0:T(4,128)(2,1)S(1)}, bf16[1,70,3,128]{3,2,1,0:T(4,128)(2,1)S(1)}, u32[]{:S(2)}, u32[]{:S(2)}) collective-permute-start(bf16[1,70,3,128]{3,2,1,0:T(4,128)(2,1)S(1)} %get-tuple-element.234), channel_id=1, source_target_pairs={{4,0},{8,4},{12,8},{0,12},{5,1},{9,5},{13,9},{1,13},{6,2},{10,6},{... | collective-permute-start | bytes 161288 | tf_op jit(solution)/shard_map/ppermute | solution.py:23
  510.7 4.9 copy-start.5
  (15 other events, 42.4 us)
Sparse Core Ops, SparseCore 0:
  386.7 31.4 all-reduce.6
  420.7 35.5 all-reduce.8
